TPU v7x, 32 devices: a whole 2x2x4 slice. The times are simulated.
32 devices in a mesh: obs: 8 (over z, core), state: 4 (over y, x).
Axes of the slice: x: 2, y: 2, z: 4, core: 2. Of those that a mesh axis runs over, the one named last changes fastest.
Arguments:
- ensemble: bfloat16 [4, 1024, 256], P('state'), may hold values from -16 to 16
- obs_values: float32 [16384], P('obs'), may hold values from -72 to 72
- obs_error: float32 [16384], P('obs'), may hold values from 6 to 24
- h_blocks: bfloat16 [8, 4, 64, 128, 128], P('obs', 'state'), may hold values from -0.125 to 0.125
- block_rows: int32 [8, 4, 64], P('obs', 'state'), may hold values from 0 to 15
- block_cols: int32 [8, 4, 64], P('obs', 'state'), may hold values from 0 to 7
- block_count: int32 [8, 4], P('obs', 'state'), may hold values from 32 to 64, as said below
Outputs:
- analysis: bfloat16 [4, 1024, 256], P('state', 'obs')
Inputs may be any that keep to these rules, and one draw needn't show every extreme that they name: `block_count`: some device has exactly 64 live slots in every draw.
All inputs are finite; a program needn't handle non-finite values.
Results may differ from a plain program's by a relative error of at most 0.009.
Values sent between devices are 32-bit elements; how exact they have to be, the bound alone decides.
A program may use at most 64 MiB of HBM per device.

v0:
```python
import math
import jax
import jax.numpy as jnp
from jax import lax
from jax.sharding import PartitionSpec as P

K = 256
BS = 128
M_DEV = 2048
BLK_DEV = 64


def on_device(ensemble, obs_values, obs_error, h_blocks, block_rows, block_cols, block_count):
    members = ensemble[0]
    slab_rows = members.shape[0]
    state_blocks = slab_rows // BS
    obs_blocks = M_DEV // BS
    member_blocks = members.reshape(state_blocks, BS, K)
    group_size = math.gcd(BLK_DEV, 32)
    group_count = BLK_DEV // group_size
    all_blocks = h_blocks[0, 0]
    all_cols = block_cols[0, 0]
    all_rows = block_rows[0, 0]
    live_count = block_count[0, 0]
    block_ids = jnp.arange(obs_blocks, dtype=jnp.int32)

    def add_group(group_index, carry):
        start = (group_index * group_size).astype(jnp.int32)
        blocks = lax.dynamic_slice_in_dim(all_blocks, start, group_size, 0)
        cols = lax.dynamic_slice_in_dim(all_cols, start, group_size, 0)
        rows = lax.dynamic_slice_in_dim(all_rows, start, group_size, 0)
        live_mask = start + jnp.arange(group_size, dtype=jnp.int32) < live_count
        picked = member_blocks[cols]
        products = jnp.einsum("bij,bjk->bik", blocks, picked, preferred_element_type=jnp.float32)
        upper_part = products.astype(jnp.bfloat16)
        lower_part = (products - upper_part.astype(jnp.float32)).astype(jnp.bfloat16)
        onehot = ((rows[None, :] == block_ids[:, None]) & live_mask[None, :]).astype(jnp.bfloat16)
        carry = carry + jnp.einsum(
            "mb,bik->mik", onehot, upper_part, preferred_element_type=jnp.float32
        )
        carry = carry + jnp.einsum(
            "mb,bik->mik", onehot, lower_part, preferred_element_type=jnp.float32
        )
        return carry

    accumulated = lax.fori_loop(
        0, group_count, add_group, jnp.zeros((obs_blocks, BS, K), jnp.float32)
    )
    slab_term = accumulated.reshape(M_DEV, K)
    state_devices = lax.axis_size("state")
    rows_share = M_DEV // state_devices
    row_offset = lax.axis_index("state") * rows_share
    own_rows = lax.psum_scatter(slab_term, "state", scatter_dimension=0, tiled=True)
    own_values = lax.dynamic_slice_in_dim(obs_values, row_offset, rows_share, 0)
    own_errors = lax.dynamic_slice_in_dim(obs_error, row_offset, rows_share, 0)
    obs_mean = jnp.mean(own_rows, axis=1)
    whitened = (own_rows - obs_mean[:, None]) / own_errors[:, None]
    innovation = (own_values - obs_mean) / own_errors
    gram_part = lax.dot_general(
        whitened, whitened, (((0,), (0,)), ((), ())), precision=lax.Precision.HIGHEST
    )
    projected_part = jnp.dot(innovation, whitened, precision=lax.Precision.HIGHEST)
    identity = jnp.eye(K, dtype=jnp.float32)
    gram_sum, projected_innovation = lax.psum((gram_part, projected_part), ("obs", "state"))
    lower_factor = jnp.linalg.cholesky(gram_sum + (K - 1) * identity)
    halfway = lax.linalg.triangular_solve(
        lower_factor, projected_innovation[:, None], left_side=True, lower=True
    )
    mean_weight = lax.linalg.triangular_solve(
        lower_factor, halfway, left_side=True, lower=True, transpose_a=True
    )
    root_inverse = lax.linalg.triangular_solve(
        lower_factor, identity, left_side=True, lower=True, transpose_a=True
    )
    transform = (math.sqrt(K - 1) * root_inverse + mean_weight).astype(jnp.bfloat16)
    piece_rows = slab_rows // lax.axis_size("obs")
    own_piece = lax.dynamic_slice_in_dim(
        members, lax.axis_index("obs") * piece_rows, piece_rows, 0
    ).astype(jnp.float32)
    state_mean = jnp.mean(own_piece, axis=1)
    anomalies = (own_piece - state_mean[:, None]).astype(jnp.bfloat16)
    analysis = state_mean[:, None] + jnp.dot(
        anomalies, transform, preferred_element_type=jnp.float32
    )
    return analysis.astype(jnp.bfloat16)[None]


def solution(mesh):
    placed = (
        P("state", None, None),
        P("obs"),
        P("obs"),
        P("obs", "state", None, None, None),
        P("obs", "state", None),
        P("obs", "state", None),
        P("obs", "state"),
    )
    return jax.shard_map(
        on_device, mesh=mesh, in_specs=placed, out_specs=P("state", "obs", None), check_vma=False
    )
```

profile of v0, /device:TPU:0, one launch (start us, length us, event | category | flops | bytes accessed | tf_op | source)
XLA Modules:
  0.0 278.9 jit_solution(10647405630408804250)
XLA Ops:
  6.5 24.7 %while.16 = (s32[]{:T(128)}, f32[16,128,256]{2,0,1:T(8,128)}, s32[64]{0:T(128)}, s32[]{:T(128)}, bf16[64,128,128]{2,1,0:T(8,128)(2,1)}, /*index=5*/s32[64]{0:T(1...) while((s32[]{:T(128)}, f32[16,128,256]{2,0,1:T(8,128)}, ...), condition=%wide.region_2.0_spmd.clone, body=%wide.region_1.0_spmd.clone.sunk | while | flops 341314720 | bytes 24123700 | solution.py:46
  6.5 0.7 compare_select_fusion.2
  7.3 1.7 gather_fusion
  9.0 3.2 %subtract_convert_fusion.2 = (bf16[32,128,256]{2,1,0:T(8,128)(2,1)S(1)}, bf16[32,128,256]{2,1,0:T(8,128)(2,1)}) fusion(bf16[32,128,256]{2,1,0:T(8,128)(2,1)S(1)} %gather_fusion, bf16[64,128,128]{2,1,0:T(8,128)(2,1)} %get-tuple-element.322, s32[]{:T(128)S(6)} %select_n.37), kind=kOutput, calls=%fused_computation.4.clone.1 | convolution fusion | flops 272629760 | bytes 7340036 | tf_op jit(solution)/shard_map/while/body/eval_jaxpr/bij,bjk->bik/dot_general | solution.py:34
  13.0 1.3 fusion.80
  14.2 4.3 %fusion.81 = f32[16,128,256]{2,0,1:T(8,128)} fusion(f32[16,128,256]{2,0,1:T(8,128)S(1)} %fusion.80, f32[16,128,256]{2,0,1:T(8,128)} %get-tuple-element.308, bf16[32,128,256]{2,1,0:T(8,128)(2,1)} %get-tuple-element.295, pred[]{:T(512)S(6)} %compare.30, s32[32]{0:T(128)S(1)} %dynamic_slice.54, pred[32]{0:T(512)(128)(4,1)S(1)} %add_compare_fusion.2), kind=kOutput, calls=%fused_computation.10.clone.1 | convolution fusion | flops 35128320 | bytes 8388769 | tf_op jit(solution)/shard_map/while/body/eval_jaxpr/mb,bik->mik/dot_general | solution.py:38
  18.6 0.7 compare_select_fusion.2
  19.3 1.7 gather_fusion
  21.0 3.2 %subtract_convert_fusion.2 = (bf16[32,128,256]{2,1,0:T(8,128)(2,1)S(1)}, bf16[32,128,256]{2,1,0:T(8,128)(2,1)}) fusion(bf16[32,128,256]{2,1,0:T(8,128)(2,1)S(1)} %gather_fusion, bf16[64,128,128]{2,1,0:T(8,128)(2,1)} %get-tuple-element.322, s32[]{:T(128)S(6)} %select_n.37), kind=kOutput, calls=%fused_computation.4.clone.1 | convolution fusion | flops 272629760 | bytes 7340036 | tf_op jit(solution)/shard_map/while/body/eval_jaxpr/bij,bjk->bik/dot_general | solution.py:34
  25.0 1.3 fusion.80
  26.3 5.0 %fusion.81 = f32[16,128,256]{2,0,1:T(8,128)} fusion(f32[16,128,256]{2,0,1:T(8,128)S(1)} %fusion.80, f32[16,128,256]{2,0,1:T(8,128)} %get-tuple-element.308, bf16[32,128,256]{2,1,0:T(8,128)(2,1)} %get-tuple-element.295, pred[]{:T(512)S(6)} %compare.30, s32[32]{0:T(128)S(1)} %dynamic_slice.54, pred[32]{0:T(512)(128)(4,1)S(1)} %add_compare_fusion.2), kind=kOutput, calls=%fused_computation.10.clone.1 | convolution fusion | flops 35128320 | bytes 8388769 | tf_op jit(solution)/shard_map/while/body/eval_jaxpr/mb,bik->mik/dot_general | solution.py:38
  31.2 4.1 %copy.18 = f32[16,128,256]{2,1,0:T(8,128)} copy(f32[16,128,256]{2,0,1:T(8,128)} %get-tuple-element.144) | data formatting | bytes 4194304 | tf_op jit(solution)/shard_map/while | solution.py:46
  35.4 0.9 convert_reduce_fusion
  36.4 37.0 %reduce-scatter.2.cloned.1.call-done = f32[512,256]{1,0:T(8,128)} async-done(((f32[2048,256]{1,0:T(8,128)}), f32[512,256]{1,0:T(8,128)}) %reduce-scatter.2.cloned.1.call-update) | async-done | bytes 524304 | tf_op jit(solution)/shard_map/reduce_scatter | solution.py:53
  73.4 1.3 reduce_sum.19
  74.7 0.8 subtract_divide_fusion.1
  75.5 3.2 %fusion.54 = f32[256,256]{0,1:T(8,128)} fusion(f32[512,256]{1,0:T(8,128)} %reduce-scatter.2.cloned.1.call-done, f32[512]{0:T(512)S(1)} %get-tuple-element.216, f32[512]{0:T(512)S(1)} %get-tuple-element.217), kind=kOutput, calls=%fused_computation.89 | convolution fusion | flops 402915328 | bytes 790528 | tf_op jit(solution)/shard_map/dot_general | solution.py:59
  79.2 39.5 %psum.15 = f32[256]{0:T(256)S(1)} all-reduce(f32[256]{0:T(256)S(1)} %bitcast.108), channel_id=1, replica_groups=mesh['obs'=8,'state'=4] {'obs','state'}, use_global_device_ids=true, to_apply=%region_10.11 | all-reduce | flops 256 | bytes 2048 | tf_op jit(solution)/shard_map/psum | solution.py:64
  118.6 87.0 %all-reduce.3.cloned.1.call-done = f32[256,256]{0,1:T(8,128)} async-done(((f32[256,256]{0,1:T(8,128)}), f32[256,256]{0,1:T(8,128)}) %all-reduce.3.cloned.1.call-update) | async-done | bytes 262160 | tf_op jit(solution)/shard_map/psum | solution.py:64
  205.6 1.0 select_add_fusion.1
  206.7 1.0 fusion.28
  207.7 11.7 %cholesky.49 = f32[128,128]{1,0:T(8,128)S(1)} custom-call(f32[128,128]{1,0:T(8,128)S(1)} %cholesky.115), custom_call_target="Cholesky" | custom-call | tf_op jit(solution)/shard_map/jit(cholesky)/cholesky | solution.py:65
  219.5 9.8 %custom-call.18 = f32[1,128,128]{1,2,0:T(8,128)S(1)} custom-call(f32[1,128,128]{2,1,0:T(8,128)S(1)} %get-tuple-element.214), custom_call_target="InvertDiagBlocksLowerTriangular" | custom-call | tf_op jit(solution)/shard_map/jit(cholesky)/cholesky | solution.py:65
  229.8 11.7 %cholesky.103 = f32[128,128]{1,0:T(8,128)S(1)} custom-call(f32[128,128]{1,0:T(8,128)S(1)} %convolution_subtract_fusion.1), custom_call_target="Cholesky" | custom-call | tf_op jit(solution)/shard_map/jit(cholesky)/cholesky | solution.py:65
  241.9 0.7 compare_reduce_fusion
  244.0 4.3 %while.15 = (s32[]{:T(128)}, f32[256,256]{0,1:T(8,128)S(1)}, s32[2,2]{1,0:T(2,128)S(1)}, f32[2,128,128]{2,1,0:T(8,128)S(1)}, s32[]{:T(128)}) while((s32[]{:T(128)}, f32[256,256]{0,1:T(8,128)S(1)}, s32[2,2]{1,0:T(2,128)S(1)}, f32[2,128,128]{2,1,0:T(8,128)S(1)}, s32[]{:T(128)}) %tuple.58), condition=%wide.while_cond, body=%wide.while_body.sunk | while | flops 2 | bytes 393321 | solution.py:72
  244.0 0.7 fusion.74
  244.6 1.3 dynamic-slice.8
  246.1 0.7 fusion.74
  246.8 1.3 dynamic-slice.8
  248.3 19.9 %custom-call.19 = f32[2,128,128]{1,2,0:T(8,128)S(1)} custom-call(f32[2,128,128]{2,1,0:T(8,128)S(1)} %get-tuple-element.152), custom_call_target="InvertDiagBlocksLowerTriangular" | custom-call | tf_op jit(solution)/shard_map/triangular_solve | solution.py:72
  270.3 1.7 fusion.21
  (52 shorter events, 5.4 us)
Async XLA Ops:
  6.5 66.9 %reduce-scatter.2.cloned.1.call-start = ((), (), s32[]{:S(2)}) async-start(), calls=%async_computation.1 | async-start | bytes 2621440 | tf_op jit(solution)/shard_map/reduce_scatter | solution.py:53
  9.0 3.2 %copy-start.1 = (s32[64]{0:T(128)S(1)}, s32[64]{0:T(128)}, u32[]{:S(2)}) copy-start(s32[64]{0:T(128)} %get-tuple-element.320) | copy-start | bytes 772 | tf_op jit(solution)/shard_map/while
  21.0 3.2 %copy-start.1 = (s32[64]{0:T(128)S(1)}, s32[64]{0:T(128)}, u32[]{:S(2)}) copy-start(s32[64]{0:T(128)} %get-tuple-element.320) | copy-start | bytes 772 | tf_op jit(solution)/shard_map/while
  35.4 170.3 %all-reduce.3.cloned.1.call-start = ((), (), s32[]{:S(2)}) async-start(), calls=%async_computation.2 | async-start | bytes 524288 | tf_op jit(solution)/shard_map/psum | solution.py:64
  73.4 5.3 %copy-start = (f32[512,256]{1,0:T(8,128)S(1)}, f32[512,256]{1,0:T(8,128)}, u32[]{:S(2)}) copy-start(f32[512,256]{1,0:T(8,128)} %reduce-scatter.2.cloned.1.call-done) | copy-start | bytes 1572868
Sparse Core Ops, SparseCore 0:
  35.5 37.9 reduce-scatter.1
  78.9 126.6 all-reduce.2
where the time goes:
time: 280 us; the launch traced here: 279 us
  waiting for transfers between devices  124 us (44%)
  other arithmetic  61.7 us (22%)
  blocking collectives  39.5 us (14%)
  matrix products  26.2 us (9%)
  between operations  14.9 us (5%)
  local copies, waits for them, and re-layouts  12.4 us (4%)
    psum x1, waiting for transfers between devices, on_device(): lax.psum((gram_part, projected_part), ('obs', 'state'))  87 us
    psum x1, blocking collectives, on_device(): lax.psum((gram_part, projected_part), ('obs', 'state'))  39.5 us
    reduce_scatter x1, waiting for transfers between devices, on_device(): lax.psum_scatter(slab_term, 'state', scatter_dimension=0, tiled=True)  37 us
    another operation x6, other arithmetic, on_device(): lower_factor = jnp.linalg.cholesky(gram_sum + (K - 1) * identity)  34 us
    another operation x3, other arithmetic, on_device(): lax.linalg.triangular_solve(lower_factor, identity, left_side=True, lower...  19.9 us
    dot_general x2, matrix products, add_group(): jnp.einsum('mb,bik->mik', onehot, upper_part, preferred_element_type=jnp....  9.29 us
    dot_general x2, matrix products, add_group(): jnp.einsum('bij,bjk->bik', blocks, picked, preferred_element_type=jnp.flo...  6.45 us
  transfers between devices with their start and end apart: 2, of which 2 were waited for; matrix products, arithmetic and copies ran while one was open for 1% of the time, Pallas kernels for 0%

commit v1 on v0

--- a/solution.py
+++ b/solution.py
@@ -61,7 +61,7 @@
     )
     projected_part = jnp.dot(innovation, whitened, precision=lax.Precision.HIGHEST)
     identity = jnp.eye(K, dtype=jnp.float32)
-    gram_sum, projected_innovation = lax.psum((gram_part, projected_part), ("obs", "state"))
+    gram_sum, projected_innovation = lax.psum(lax.psum((gram_part, projected_part), "state"), "obs")
     lower_factor = jnp.linalg.cholesky(gram_sum + (K - 1) * identity)
     halfway = lax.linalg.triangular_solve(
         lower_factor, projected_innovation[:, None], left_side=True, lower=True

time: 280 us -> 253 us (0.904)
  blocking collectives: 39.5 us -> 23 us
  waiting for transfers between devices: 124 us -> 115 us
    psum x1 -> x2, blocking collectives: 39.5 us -> 23 us  [the longest x1 14.1 us: on_device(): lax.psum(lax.psum((gram_part, projected_part), 'state'), 'obs')]
    psum x1 -> x2, waiting for transfers between devices: 87 us -> 76.5 us  [the longest x1 42.2 us: on_device(): lax.psum((gram_part, projected_part), 'state')]
  transfers between devices with their start and end apart: 2 -> 3, of which waited for: 2 -> 3; matrix products, arithmetic and copies ran while one was open for 1% -> 1% of each run, Pallas kernels for 0% -> 0%
where the time goes in v1:
time: 253 us
  waiting for transfers between devices  115 us (45%)
  other arithmetic  61.7 us (24%)
  matrix products  26.2 us (10%)
  blocking collectives  23 us (9%)
  between operations  14.6 us (6%)
  local copies, waits for them, and re-layouts  12.4 us (5%)
    psum x1, waiting for transfers between devices, on_device(): lax.psum((gram_part, projected_part), 'state')  42.2 us
    reduce_scatter x1, waiting for transfers between devices, on_device(): lax.psum_scatter(slab_term, 'state', scatter_dimension=0, tiled=True)  38 us
    psum x1, waiting for transfers between devices, on_device(): lax.psum(lax.psum((gram_part, projected_part), 'state'), 'obs')  34.3 us
    another operation x6, other arithmetic, on_device(): lower_factor = jnp.linalg.cholesky(gram_sum + (K - 1) * identity)  34 us
    another operation x3, other arithmetic, on_device(): lax.linalg.triangular_solve(lower_factor, identity, left_side=True, lower...  19.9 us
    psum x1, blocking collectives, on_device(): lax.psum(lax.psum((gram_part, projected_part), 'state'), 'obs')  14.1 us
    dot_general x2, matrix products, add_group(): jnp.einsum('mb,bik->mik', onehot, upper_part, preferred_element_type=jnp....  9.29 us
    psum x1, blocking collectives, on_device(): lax.psum((gram_part, projected_part), 'state')  8.96 us
  transfers between devices with their start and end apart: 3, of which 3 were waited for; matrix products, arithmetic and copies ran while one was open for 1% of the time, Pallas kernels for 0%

profile of v1, /device:TPU:0, one launch (start us, length us, event | category | flops | bytes accessed | tf_op | source)
XLA Modules:
  0.0 252.7 jit_solution(10752231702190541496)
XLA Ops:
  6.5 24.7 %while.16 = (s32[]{:T(128)}, f32[16,128,256]{2,0,1:T(8,128)}, s32[64]{0:T(128)}, s32[]{:T(128)}, bf16[64,128,128]{2,1,0:T(8,128)(2,1)}, /*index=5*/s32[64]{0:T(1...) while((s32[]{:T(128)}, f32[16,128,256]{2,0,1:T(8,128)}, ...), condition=%wide.region_2.0_spmd.clone, body=%wide.region_1.0_spmd.clone.sunk | while | flops 341314720 | bytes 24123700 | solution.py:46
  6.5 0.7 compare_select_fusion.2
  7.3 1.7 gather_fusion
  9.0 3.2 %subtract_convert_fusion.2 = (bf16[32,128,256]{2,1,0:T(8,128)(2,1)S(1)}, bf16[32,128,256]{2,1,0:T(8,128)(2,1)}) fusion(bf16[32,128,256]{2,1,0:T(8,128)(2,1)S(1)} %gather_fusion, bf16[64,128,128]{2,1,0:T(8,128)(2,1)} %get-tuple-element.322, s32[]{:T(128)S(6)} %select_n.37), kind=kOutput, calls=%fused_computation.4.clone.1 | convolution fusion | flops 272629760 | bytes 7340036 | tf_op jit(solution)/shard_map/while/body/eval_jaxpr/bij,bjk->bik/dot_general | solution.py:34
  13.0 1.3 fusion.80
  14.2 4.3 %fusion.81 = f32[16,128,256]{2,0,1:T(8,128)} fusion(f32[16,128,256]{2,0,1:T(8,128)S(1)} %fusion.80, f32[16,128,256]{2,0,1:T(8,128)} %get-tuple-element.308, bf16[32,128,256]{2,1,0:T(8,128)(2,1)} %get-tuple-element.295, pred[]{:T(512)S(6)} %compare.30, s32[32]{0:T(128)S(1)} %dynamic_slice.54, pred[32]{0:T(512)(128)(4,1)S(1)} %add_compare_fusion.2), kind=kOutput, calls=%fused_computation.10.clone.1 | convolution fusion | flops 35128320 | bytes 8388769 | tf_op jit(solution)/shard_map/while/body/eval_jaxpr/mb,bik->mik/dot_general | solution.py:38
  18.6 0.7 compare_select_fusion.2
  19.3 1.7 gather_fusion
  21.0 3.2 %subtract_convert_fusion.2 = (bf16[32,128,256]{2,1,0:T(8,128)(2,1)S(1)}, bf16[32,128,256]{2,1,0:T(8,128)(2,1)}) fusion(bf16[32,128,256]{2,1,0:T(8,128)(2,1)S(1)} %gather_fusion, bf16[64,128,128]{2,1,0:T(8,128)(2,1)} %get-tuple-element.322, s32[]{:T(128)S(6)} %select_n.37), kind=kOutput, calls=%fused_computation.4.clone.1 | convolution fusion | flops 272629760 | bytes 7340036 | tf_op jit(solution)/shard_map/while/body/eval_jaxpr/bij,bjk->bik/dot_general | solution.py:34
  25.0 1.3 fusion.80
  26.3 5.0 %fusion.81 = f32[16,128,256]{2,0,1:T(8,128)} fusion(f32[16,128,256]{2,0,1:T(8,128)S(1)} %fusion.80, f32[16,128,256]{2,0,1:T(8,128)} %get-tuple-element.308, bf16[32,128,256]{2,1,0:T(8,128)(2,1)} %get-tuple-element.295, pred[]{:T(512)S(6)} %compare.30, s32[32]{0:T(128)S(1)} %dynamic_slice.54, pred[32]{0:T(512)(128)(4,1)S(1)} %add_compare_fusion.2), kind=kOutput, calls=%fused_computation.10.clone.1 | convolution fusion | flops 35128320 | bytes 8388769 | tf_op jit(solution)/shard_map/while/body/eval_jaxpr/mb,bik->mik/dot_general | solution.py:38
  31.2 4.1 %copy.18 = f32[16,128,256]{2,1,0:T(8,128)} copy(f32[16,128,256]{2,0,1:T(8,128)} %get-tuple-element.144) | data formatting | bytes 4194304 | tf_op jit(solution)/shard_map/while | solution.py:46
  35.4 38.0 %reduce-scatter.2.cloned.1.call-done = f32[512,256]{1,0:T(8,128)} async-done(((f32[2048,256]{1,0:T(8,128)}), f32[512,256]{1,0:T(8,128)}) %reduce-scatter.2.cloned.1.call-update) | async-done | bytes 524304 | tf_op jit(solution)/shard_map/reduce_scatter | solution.py:53
  73.4 1.3 reduce_sum.19
  74.7 0.8 subtract_divide_fusion.1
  75.5 3.2 %fusion.54 = f32[256,256]{0,1:T(8,128)} fusion(f32[512,256]{1,0:T(8,128)} %reduce-scatter.2.cloned.1.call-done, f32[512]{0:T(512)S(1)} %get-tuple-element.216, f32[512]{0:T(512)S(1)} %get-tuple-element.217), kind=kOutput, calls=%fused_computation.89 | convolution fusion | flops 402915328 | bytes 790528 | tf_op jit(solution)/shard_map/dot_general | solution.py:59
  78.8 0.9 convert_reduce_fusion
  79.8 42.2 %all-reduce.4.cloned.1.call-done = f32[256,256]{0,1:T(8,128)} async-done(((f32[256,256]{0,1:T(8,128)}), f32[256,256]{0,1:T(8,128)}) %all-reduce.4.cloned.1.call-update) | async-done | bytes 262160 | tf_op jit(solution)/shard_map/psum | solution.py:64
  122.4 9.0 %psum.30 = f32[256]{0:T(256)S(1)} all-reduce(f32[256]{0:T(256)S(1)} %bitcast.108), channel_id=1, replica_groups=mesh['obs'=8,'state'=4] {'state'}, use_global_device_ids=true, to_apply=%region_11.12 | all-reduce | flops 256 | bytes 2048 | tf_op jit(solution)/shard_map/psum | solution.py:64
  131.4 14.1 %psum.31 = f32[256]{0:T(256)S(1)} all-reduce(f32[256]{0:T(256)S(1)} %psum.30), channel_id=1, replica_groups=mesh['obs'=8,'state'=4] {'obs'}, use_global_device_ids=true, to_apply=%region_12.13 | all-reduce | flops 256 | bytes 2048 | tf_op jit(solution)/shard_map/psum | solution.py:64
  145.4 34.3 %all-reduce.6.cloned.1.call-done = f32[256,256]{0,1:T(8,128)} async-done(((f32[256,256]{0,1:T(8,128)}), f32[256,256]{0,1:T(8,128)}) %all-reduce.6.cloned.1.call-update) | async-done | bytes 262160 | tf_op jit(solution)/shard_map/psum | solution.py:64
  179.7 1.0 select_add_fusion.1
  180.9 1.0 fusion.28
  181.9 11.7 %cholesky.49 = f32[128,128]{1,0:T(8,128)S(1)} custom-call(f32[128,128]{1,0:T(8,128)S(1)} %cholesky.115), custom_call_target="Cholesky" | custom-call | tf_op jit(solution)/shard_map/jit(cholesky)/cholesky | solution.py:65
  193.6 9.8 %custom-call.18 = f32[1,128,128]{1,2,0:T(8,128)S(1)} custom-call(f32[1,128,128]{2,1,0:T(8,128)S(1)} %get-tuple-element.214), custom_call_target="InvertDiagBlocksLowerTriangular" | custom-call | tf_op jit(solution)/shard_map/jit(cholesky)/cholesky | solution.py:65
  203.9 11.7 %cholesky.103 = f32[128,128]{1,0:T(8,128)S(1)} custom-call(f32[128,128]{1,0:T(8,128)S(1)} %convolution_subtract_fusion.1), custom_call_target="Cholesky" | custom-call | tf_op jit(solution)/shard_map/jit(cholesky)/cholesky | solution.py:65
  216.0 0.7 compare_reduce_fusion
  218.1 4.3 %while.15 = (s32[]{:T(128)}, f32[256,256]{0,1:T(8,128)S(1)}, s32[2,2]{1,0:T(2,128)S(1)}, f32[2,128,128]{2,1,0:T(8,128)S(1)}, s32[]{:T(128)}) while((s32[]{:T(128)}, f32[256,256]{0,1:T(8,128)S(1)}, s32[2,2]{1,0:T(2,128)S(1)}, f32[2,128,128]{2,1,0:T(8,128)S(1)}, s32[]{:T(128)}) %tuple.58), condition=%wide.while_cond, body=%wide.while_body.sunk | while | flops 2 | bytes 393321 | solution.py:72
  218.8 1.3 dynamic-slice.8
  220.9 1.3 dynamic-slice.8
  222.4 19.9 %custom-call.19 = f32[2,128,128]{1,2,0:T(8,128)S(1)} custom-call(f32[2,128,128]{2,1,0:T(8,128)S(1)} %get-tuple-element.152), custom_call_target="InvertDiagBlocksLowerTriangular" | custom-call | tf_op jit(solution)/shard_map/triangular_solve | solution.py:72
  244.4 1.7 fusion.21
  (56 shorter events, 6.8 us)
Async XLA Ops:
  6.5 66.9 %reduce-scatter.2.cloned.1.call-start = ((), (), s32[]{:S(2)}) async-start(), calls=%async_computation.1 | async-start | bytes 2621440 | tf_op jit(solution)/shard_map/reduce_scatter | solution.py:53
  9.0 3.2 %copy-start.1 = (s32[64]{0:T(128)S(1)}, s32[64]{0:T(128)}, u32[]{:S(2)}) copy-start(s32[64]{0:T(128)} %get-tuple-element.320) | copy-start | bytes 772 | tf_op jit(solution)/shard_map/while
  21.0 3.2 %copy-start.1 = (s32[64]{0:T(128)S(1)}, s32[64]{0:T(128)}, u32[]{:S(2)}) copy-start(s32[64]{0:T(128)} %get-tuple-element.320) | copy-start | bytes 772 | tf_op jit(solution)/shard_map/while
  35.4 86.6 %all-reduce.4.cloned.1.call-start = ((), (), s32[]{:S(2)}) async-start(), calls=%async_computation.2 | async-start | bytes 524288 | tf_op jit(solution)/shard_map/psum | solution.py:64
  73.4 48.5 %copy-start = (f32[512,256]{1,0:T(8,128)S(1)}, f32[512,256]{1,0:T(8,128)}, u32[]{:S(2)}) copy-start(f32[512,256]{1,0:T(8,128)} %reduce-scatter.2.cloned.1.call-done) | copy-start | bytes 1572868
  78.7 101.0 %all-reduce.6.cloned.1.call-start = ((), (), s32[]{:S(2)}) async-start(), calls=%async_computation.3 | async-start | bytes 524288 | tf_op jit(solution)/shard_map/psum | solution.py:64
Sparse Core Ops, SparseCore 0:
  35.5 37.9 reduce-scatter.1
  78.9 43.0 all-reduce.3
  124.3 55.4 all-reduce.5
